TPU v7x, 256 devices: a whole 4x4x8 slice. The times are simulated.
256 devices in a mesh: dp: 2 (over core), ctx: 16 (over z_hi, y), exp: 8 (over x, z_lo).
Axes of the slice: x: 4, y: 4, z: 8 (z_hi: 4, z_lo: 2; z = z_hi * 2 + z_lo), core: 2. Of those that a mesh axis runs over, the one named last changes fastest.
Arguments:
- tokens: bfloat16 [2, 2048, 2560], P('dp', 'ctx'), may hold values from -6 to 6
- queries: bfloat16 [2, 2048, 16, 576], P('dp', 'ctx', 'exp'), may hold values from -240 to 240
- kv_weight: bfloat16 [2560, 576], P('exp'), may hold values from -0.125 to 0.125
- kv_gain: bfloat16 [512], replicated, may hold values from 0.5 to 1.5
- uv_weight: bfloat16 [16, 512, 128], P('exp'), may hold values from -0.75 to 0.75
- out_weight: bfloat16 [2048, 2560], P('exp'), may hold values from -0.5 to 0.5
- post_gain: bfloat16 [2560], replicated, may hold values from 0.5 to 1.5
- router_weight: bfloat16 [2560, 32], replicated, may hold values from -0.125 to 0.125
- expert_ids: int32 [2, 2048, 6], P('dp', 'ctx'), may hold values from 0 to 31, all different within a row; in each aligned block of 128 rows (0 to 127, 128 to 255, ..., all dimensions but the last counted through in order) at most 32 rows name the same one
- doc_ids: int32 [2, 2048], P('dp', 'ctx'), may hold values from 0 to 3, never falling along the last dimension, each value on 1 to 1024 neighbouring positions
- gate_weight: bfloat16 [32, 2560, 1536], P('ctx', None, 'exp'), may hold values from -0.125 to 0.125
- up_weight: bfloat16 [32, 2560, 1536], P('ctx', None, 'exp'), may hold values from -0.125 to 0.125
- down_weight: bfloat16 [32, 1536, 2560], P('ctx', 'exp'), may hold values from -0.15625 to 0.15625
- cotangent: bfloat16 [2, 2048, 2560], P('dp', 'ctx'), may hold values from -6 to 6
Outputs:
- layer_out: bfloat16 [2, 2048, 2560], P('dp', 'ctx')
- router_grad: float32 [2560, 32], replicated
- gate_grad: bfloat16 [32, 2560, 1536], P('ctx', 'dp', 'exp')
- up_grad: bfloat16 [32, 2560, 1536], P('ctx', 'dp', 'exp')
- down_grad: bfloat16 [32, 1536, 2560], P('ctx', 'exp', 'dp')
Inputs may be any that keep to these rules, and one draw needn't show every extreme that they name: `expert_ids`: in each aligned block of 128 positions of a sequence no expert is named by more than 32 of the block's assignments; the experts of one token differ. `doc_ids`: document numbers never fall along a sequence; a document has at most 1024 positions.
All inputs are finite; a program needn't handle non-finite values.
Results may differ from a plain program's by a relative error of at most 0.023.
The roundings to bfloat16 on the way count: a program that leaves them out, or rounds other values in their place, can miss the bound.
Values may be sent and summed in bfloat16 or wider, within the bound.
No kernel may reach another device: no remote copies, remote signals or barrier semaphores. Data moves between devices by JAX's collectives and lax.ppermute only.
A program may use at most 128 MiB of HBM per device.

v0:
```python
import jax
import jax.numpy as jnp
from jax import lax
from jax.sharding import PartitionSpec as P

ROPE = 64
NOPE = 128
epsilon = 1e-06


def from_everyone(array, axis):
    count = lax.axis_size(axis)
    return lax.all_to_all(
        jnp.broadcast_to(array[None], (count, *array.shape)), axis, 0, 0, tiled=True
    )


def taken_together(array, axis):
    everything = from_everyone(array, axis)
    return jnp.sum(everything, axis=0)


def in_one_piece(arrays, axis, split_dim, concat_dim, along):
    both = jnp.concatenate(arrays, axis=along)
    result, at, gathered = (
        lax.all_to_all(both, axis, split_axis=split_dim, concat_axis=concat_dim, tiled=True),
        0,
        [],
    )
    for a in arrays:
        gathered.append(lax.slice_in_dim(result, at, at + a.shape[along], axis=along))
        at += a.shape[along]
    return tuple(gathered)


def rms_scale(values, gain):
    return values * lax.rsqrt(jnp.mean(values * values, axis=-1, keepdims=True) + epsilon) * gain


def rotate(rope_part, positions):
    half_width = rope_part.shape[-1] // 2
    frequency = jnp.power(
        10000.0, -2.0 * jnp.arange(half_width, dtype=jnp.float32) / rope_part.shape[-1]
    )
    angles = positions.astype(jnp.float32)[:, None] * frequency[None, :]
    cosine = jnp.cos(angles)
    sine_part = jnp.sin(angles)
    first_half = rope_part[:, :half_width]
    second = rope_part[:, half_width:]
    return jnp.concatenate(
        [first_half * cosine - second * sine_part, second * cosine + first_half * sine_part], axis=1
    )


def route_slots(outgoing):
    moved = lax.all_to_all(outgoing, ("dp", "ctx"), split_axis=0, concat_axis=0, tiled=True)
    return moved


def local(
    tokens,
    queries,
    kv_weight,
    kv_gain,
    uv_weight,
    out_weight,
    post_gain,
    router_weight,
    expert_ids,
    doc_ids,
    gate_weight,
    up_weight,
    down_weight,
    cotangent,
):
    local_rows = tokens[0]
    seq_rows = local_rows.shape[0]
    model_width = local_rows.shape[1]
    latent_width = kv_gain.shape[0]
    row_share = kv_weight.shape[0]
    columns = lax.dynamic_slice_in_dim(local_rows, lax.axis_index("exp") * row_share, row_share, 1)
    compressed = taken_together(
        jnp.dot(columns, kv_weight, preferred_element_type=jnp.float32), "exp"
    )
    positions = lax.axis_index("ctx") * seq_rows + jnp.arange(seq_rows, dtype=jnp.int32)
    latent = rms_scale(compressed[:, :latent_width], kv_gain.astype(jnp.float32)).astype(
        jnp.bfloat16
    )
    rope_key = rotate(compressed[:, latent_width:], positions).astype(jnp.bfloat16)
    key_rows = jnp.concatenate([latent, rope_key], axis=1)
    all_keys, all_docs = (
        lax.all_gather(key_rows, "ctx", axis=0, tiled=True),
        lax.all_gather(doc_ids[0], "ctx", axis=0, tiled=True),
    )
    key_positions = jnp.arange(all_keys.shape[0], dtype=jnp.int32)
    allowed = (key_positions[None, :] <= positions[:, None]) & (
        all_docs[None, :] == doc_ids[0][:, None]
    )
    allowed = allowed[:, None, :]
    score_scale = (NOPE + ROPE) ** (-0.5)
    scores = (
        jnp.einsum("qhd,kd->qhk", queries[0], all_keys, preferred_element_type=jnp.float32)
        * score_scale
    )
    score_peak = jnp.max(jnp.where(allowed, scores, -1e30), axis=-1, keepdims=True)
    weights = jnp.exp(jnp.where(allowed, scores - score_peak, -1e30))
    weight_total = jnp.sum(weights, axis=-1, keepdims=True)
    mixed_latent = (
        jnp.einsum(
            "qhk,kl->qhl",
            weights.astype(jnp.bfloat16),
            all_keys[:, :latent_width],
            preferred_element_type=jnp.float32,
        )
        / weight_total
    )
    mixed_latent = mixed_latent.astype(jnp.bfloat16)
    head_values = (
        jnp.einsum("qhl,hlv->qhv", mixed_latent, uv_weight, preferred_element_type=jnp.float32)
        .astype(jnp.bfloat16)
        .reshape(seq_rows, -1)
    )
    head_part = jnp.dot(head_values, out_weight, preferred_element_type=jnp.float32)
    attention = lax.psum(head_part, "exp")
    hidden = (local_rows.astype(jnp.float32) + attention).astype(jnp.bfloat16)
    normed = rms_scale(hidden.astype(jnp.float32), post_gain.astype(jnp.float32)).astype(
        jnp.bfloat16
    )
    logits = jnp.dot(normed, router_weight, preferred_element_type=jnp.float32)
    router_probs = jax.nn.softmax(logits, axis=-1)
    picked_ids = expert_ids[0]
    experts_all = router_weight.shape[1]
    top_count = picked_ids.shape[1]
    chosen = jnp.take_along_axis(router_probs, picked_ids, axis=1)
    chosen_sum = jnp.sum(chosen, axis=1, keepdims=True)
    route_w = chosen / chosen_sum
    route_wb = route_w.astype(jnp.bfloat16)
    ctx_count = lax.axis_size("ctx")
    held_experts = experts_all // ctx_count
    capacity = (4 * seq_rows * top_count + 3 * experts_all - 1) // (3 * experts_all)
    flat_ids = picked_ids.reshape(-1)
    onehot = (flat_ids[:, None] == jnp.arange(experts_all, dtype=jnp.int32)[None, :]).astype(
        jnp.int32
    )
    slot_rank = jnp.sum((jnp.cumsum(onehot, axis=0) - onehot) * onehot, axis=1).reshape(
        seq_rows, top_count
    )
    dp_count = lax.axis_size("dp")
    local_count = held_experts // dp_count
    first_local = lax.axis_index("dp") * local_count
    gate_local = lax.dynamic_slice_in_dim(gate_weight, first_local, local_count, 0)
    up_local = lax.dynamic_slice_in_dim(up_weight, first_local, local_count, 0)
    down_local = lax.dynamic_slice_in_dim(down_weight, first_local, local_count, 0)
    home_ctx = picked_ids // held_experts
    remainder = picked_ids % held_experts
    home_dp = remainder // local_count
    within = remainder % local_count
    slot_index = ((home_dp * ctx_count + home_ctx) * local_count + within) * capacity + slot_rank
    slot_hits = (
        slot_index[:, :, None] == jnp.arange(experts_all * capacity, dtype=jnp.int32)[None, None, :]
    )
    dispatch = jnp.any(slot_hits, axis=1).astype(jnp.bfloat16)
    combine = jnp.sum(
        jnp.where(slot_hits, route_wb[:, :, None], jnp.zeros((), jnp.bfloat16)), axis=1
    )
    outgoing = jnp.einsum("se,sd->ed", dispatch, normed, preferred_element_type=jnp.float32).astype(
        jnp.bfloat16
    )
    outgoing = outgoing.reshape(-1, local_count, capacity, model_width)
    arrived = route_slots(outgoing)
    gate_pre = jnp.einsum("sjcd,jdf->sjcf", arrived, gate_local, preferred_element_type=jnp.float32)
    up_pre = jnp.einsum("sjcd,jdf->sjcf", arrived, up_local, preferred_element_type=jnp.float32)
    activated = (jax.nn.silu(gate_pre) * up_pre).astype(jnp.bfloat16)
    expert_part = jnp.einsum(
        "sjcf,jfd->sjcd", activated, down_local, preferred_element_type=jnp.float32
    ).astype(jnp.bfloat16)
    returned = lax.all_to_all(expert_part, ("dp", "ctx"), split_axis=0, concat_axis=0, tiled=True)
    returned = returned.reshape(experts_all * capacity, model_width)
    moe_part = jnp.dot(combine, returned, preferred_element_type=jnp.float32)
    cot_rows = cotangent[0]
    cross_terms = jnp.einsum("sd,ed->se", cot_rows, returned, preferred_element_type=jnp.float32)
    dweight_part = jnp.take_along_axis(cross_terms, slot_index, axis=1)
    moe, dweight = lax.psum((moe_part, dweight_part), "exp")
    layer_out = (hidden.astype(jnp.float32) + moe).astype(jnp.bfloat16)
    mean_term = jnp.sum(dweight * route_w, axis=1, keepdims=True)
    dchosen = (dweight - mean_term) / chosen_sum
    id_hits = (
        picked_ids[:, :, None] == jnp.arange(experts_all, dtype=jnp.int32)[None, None, :]
    ).astype(jnp.float32)
    dprobs = jnp.sum(id_hits * dchosen[:, :, None], axis=1)
    dlogits = router_probs * (dprobs - jnp.sum(router_probs * dprobs, axis=1, keepdims=True))
    router_term = jnp.dot(normed.astype(jnp.float32).T, dlogits, precision=lax.Precision.HIGHEST)
    router_grad = lax.psum(router_term, ("dp", "ctx"))
    slot_cot = jnp.einsum(
        "se,sd->ed", combine, cot_rows, preferred_element_type=jnp.float32
    ).astype(jnp.bfloat16)
    slot_cot = slot_cot.reshape(-1, local_count, capacity, model_width)
    cot_arrived = route_slots(slot_cot)
    down_term = jnp.einsum(
        "sjcf,sjcd->jfd", activated, cot_arrived, preferred_element_type=jnp.float32
    )
    dact = jnp.einsum("sjcd,jfd->sjcf", cot_arrived, down_local, preferred_element_type=jnp.float32)
    sigmoid_gate = jax.nn.sigmoid(gate_pre)
    dgate = (dact * up_pre * sigmoid_gate * (1.0 + gate_pre * (1.0 - sigmoid_gate))).astype(
        jnp.bfloat16
    )
    dup = (dact * gate_pre * sigmoid_gate).astype(jnp.bfloat16)
    gate_term = jnp.einsum("sjcd,sjcf->jdf", arrived, dgate, preferred_element_type=jnp.float32)
    up_term = jnp.einsum("sjcd,sjcf->jdf", arrived, dup, preferred_element_type=jnp.float32)
    gate_out, up_out = in_one_piece(
        (gate_term.astype(jnp.bfloat16), up_term.astype(jnp.bfloat16)), "dp", 1, 0, 2
    )
    down_out = lax.all_to_all(
        down_term.astype(jnp.bfloat16), "dp", split_axis=2, concat_axis=0, tiled=True
    )
    return (layer_out[None], router_grad, gate_out, up_out, down_out)


def solution(mesh):
    placed = (
        P("dp", "ctx", None),
        P("dp", "ctx", "exp", None),
        P("exp", None),
        P(),
        P("exp", None, None),
        P("exp", None),
        P(),
        P(),
        P("dp", "ctx", None),
        P("dp", "ctx"),
        P("ctx", None, "exp"),
        P("ctx", None, "exp"),
        P("ctx", "exp", None),
        P("dp", "ctx", None),
    )
    return jax.shard_map(
        local,
        mesh=mesh,
        in_specs=placed,
        out_specs=(
            P("dp", "ctx", None),
            P(),
            P("ctx", "dp", "exp"),
            P("ctx", "dp", "exp"),
            P("ctx", "exp", "dp"),
        ),
        check_vma=False,
    )
```

profile of v0, /device:TPU:88, one launch (start us, length us, event | category | flops | bytes accessed | tf_op | source)
XLA Modules:
  0.0 998.6 jit_solution(10595866600486797685)
XLA Ops:
  10.4 5.8 all-to-all-start
  16.3 29.8 %all-to-all-done = f32[8,128,576]{1,2,0:T(8,128)} async-done(((f32[8,128,576]{1,2,0:T(8,128)}), f32[8,128,576]{1,2,0:T(8,128)}, u32[]{:S(2)}, u32[]{:S(2)}) %all-to-all-start) | async-done | bytes 2359328 | tf_op jit(solution)/shard_map/all_to_all | solution.py:13
  46.0 1.8 reduce_sum.102
  49.0 37.8 %all-gather = s32[1,2048]{1,0:T(1,128)S(1)} all-gather(s32[1,128]{1,0:T(1,128)S(1)} %copy-done.4), channel_id=2, replica_groups=mesh['dp'=2,'ctx'=16,'exp'=8] {'ctx'}, dimensions={1}, use_global_device_ids=true | all-gather | bytes 8704 | tf_op jit(solution)/shard_map/all_gather | solution.py:93
  87.1 26.5 %all-gather.3.cloned.1.call-done = bf16[2048,576]{0,1:T(8,128)(2,1)} async-done(((bf16[128,576]{0,1:T(8,128)(2,1)}), bf16[2048,576]{0,1:T(8,128)(2,1)}) %all-gather.3.cloned.1.call-update) | async-done | bytes 2359312 | tf_op jit(solution)/shard_map/all_gather | solution.py:92
  113.6 2.7 fusion.51
  116.3 1.9 fusion.156
  118.3 2.9 fusion.72
  123.1 1.7 reduce-window.6
  126.0 83.0 %all-reduce.4.cloned.1.call-done = f32[128,2560]{1,0:T(8,128)} async-done(((f32[128,2560]{1,0:T(8,128)}), f32[128,2560]{1,0:T(8,128)}) %all-reduce.4.cloned.1.call-update) | async-done | bytes 1310736 | tf_op jit(solution)/shard_map/psum | solution.py:124
  209.0 1.8 fusion.64
  210.8 3.9 convolution_convert_fusion.2
  214.7 8.9 all-to-all-start.1
  223.7 113.3 %all-to-all-done.1 = bf16[32,1,32,2560]{3,2,1,0:T(8,128)(2,1)} async-done(((bf16[32,1,32,2560]{3,2,1,0:T(8,128)(2,1)}), bf16[32,1,32,2560]{3,2,1,0:T(8,128)(2,1)}, u32[]{:S(2)}, u32[]{:S(2)}) %all-to-all-start.1) | async-done | bytes 5242912 | tf_op jit(solution)/shard_map/all_to_all | solution.py:56
  336.9 4.4 fusion.55
  341.4 5.4 multiply_convert_fusion.2
  347.6 3.8 fusion.13
  351.4 12.1 %all-to-all-start.2 = ((bf16[32,1,32,2560]{3,2,1,0:T(8,128)(2,1)}), bf16[32,1,32,2560]{3,2,1,0:T(8,128)(2,1)}, u32[]{:S(2)}, u32[]{:S(2)}) async-start(bf16[32,1,32,2560]{3,2,1,0:T(8,128)(2,1)} %fusion.13), calls=%async_computation.2 | async-start | bytes 10485760 | tf_op jit(solution)/shard_map/all_to_all | solution.py:177
  364.6 5.1 gather_fusion
  370.0 107.0 %all-to-all-done.2 = bf16[32,1,32,2560]{3,2,1,0:T(8,128)(2,1)} async-done(((bf16[32,1,32,2560]{3,2,1,0:T(8,128)(2,1)}), bf16[32,1,32,2560]{3,2,1,0:T(8,128)(2,1)}, u32[]{:S(2)}, u32[]{:S(2)}) %all-to-all-start.2) | async-done | bytes 5242912 | tf_op jit(solution)/shard_map/all_to_all | solution.py:177
  477.0 4.1 convolution_bitcast_fusion
  481.1 5.1 gather_fusion.1
  486.4 23.5 %psum.30 = f32[128,6]{0,1:T(8,128)S(1)} all-reduce(f32[128,6]{0,1:T(8,128)S(1)} %and_select_fusion), channel_id=1, replica_groups=mesh['dp'=2,'ctx'=16,'exp'=8] {'exp'}, use_global_device_ids=true, to_apply=%region_15.16 | all-reduce | flops 768 | bytes 6144 | tf_op jit(solution)/shard_map/psum | solution.py:183
  510.4 5.0 convolution_convert_fusion
  515.4 9.6 all-to-all-start.3
  525.0 4.4 fusion.159
  530.9 158.4 %all-reduce.6.cloned.1.call-done = f32[128,2560]{1,0:T(8,128)} async-done(((f32[128,2560]{1,0:T(8,128)}), f32[128,2560]{1,0:T(8,128)}) %all-reduce.6.cloned.1.call-update) | async-done | bytes 1310736 | tf_op jit(solution)/shard_map/psum | solution.py:183
  689.3 2.3 fusion.86
  691.6 4.1 fusion.61
  695.8 3.9 fusion.38
  699.6 3.8 fusion.35
  704.9 8.9 copy.117
  714.4 18.2 %reduce.3 = bf16[2560,384]{1,0:T(8,128)(2,1)} reduce(bf16[2560,1,384]{2,1,0:T(2,128)(2,1)} %bitcast.237, bf16[]{:T(256)} %broadcast.489), dimensions={1}, to_apply=%bitcast.212.reduce_sub_computation | reduce | bytes 3932162
  732.6 2.8 reshape.425
  735.3 8.4 all_to_all.50
  743.7 4.2 reshape.426
  748.0 2.5 copy.128
  750.5 4.7 fusion.32
  756.8 2.3 copy.120
  760.5 6.3 copy.118
  766.8 15.4 %reduce.4 = bf16[2560,192]{1,0:T(8,128)(2,1)S(1)} reduce(bf16[2560,1,192]{2,1,0:T(2,128)(2,1)} %bitcast.241, bf16[]{:T(256)} %broadcast.489), dimensions={1}, to_apply=%bitcast.214.reduce_sub_computation | reduce | bytes 1966082
  782.1 2.3 reshape.427
  784.5 5.6 all_to_all.51
  790.1 2.9 reshape.428
  793.0 5.1 copy.119
  799.3 2.2 copy.122
  801.5 188.8 %all-reduce.8.cloned.1.call-done = f32[2560,32]{0,1:T(8,128)} async-done(((f32[2560,32]{0,1:T(8,128)}), f32[2560,32]{0,1:T(8,128)}) %all-reduce.8.cloned.1.call-update) | async-done | bytes 327696 | tf_op jit(solution)/shard_map/psum | solution.py:193
  990.4 1.7 copy.146
  (88 shorter events, 17.9 us)
Async XLA Ops:
  7.2 340.4 %copy-start = (bf16[2,192,2560]{2,1,0:T(8,128)(2,1)S(1)}, bf16[2,192,2560]{2,1,0:T(8,128)(2,1)}, u32[]{:S(2)}) copy-start(bf16[2,192,2560]{2,1,0:T(8,128)(2,1)} %param.26) | copy-start | bytes 5898244
  10.4 5.9 copy-start.5
  10.4 35.7 %all-to-all-start = ((f32[8,128,576]{1,2,0:T(8,128)}), f32[8,128,576]{1,2,0:T(8,128)}, u32[]{:S(2)}, u32[]{:S(2)}) async-start(f32[8,128,576]{1,2,0:T(8,128)} %broadcast_in_dim.34), calls=%async_computation | async-start | bytes 4718592 | tf_op jit(solution)/shard_map/all_to_all | solution.py:13
  16.1 32.8 %copy-start.4 = (s32[1,128]{1,0:T(1,128)S(1)}, s32[1,128]{1,0:T(1,128)}, u32[]{:S(2)}) copy-start(s32[1,128]{1,0:T(1,128)} %param.23) | copy-start | bytes 1540
  16.2 97.5 %copy-start.7 = (bf16[1,128,2,576]{1,3,2,0:T(8,128)(2,1)S(1)}, bf16[1,128,2,576]{1,3,2,0:T(8,128)(2,1)}, u32[]{:S(2)}) copy-start(bf16[1,128,2,576]{1,3,2,0:T(8,128)(2,1)} %param.15) | copy-start | bytes 884740
  16.2 97.4 %all-gather.3.cloned.1.call-start = ((), (), s32[]{:S(2)}) async-start(), calls=%async_computation.6 | async-start | bytes 2506752 | tf_op jit(solution)/shard_map/all_gather | solution.py:92
  48.9 160.1 %all-reduce.4.cloned.1.call-start = ((), (), s32[]{:S(2)}) async-start(), calls=%async_computation.7 | async-start | bytes 2621440 | tf_op jit(solution)/shard_map/psum | solution.py:124
  118.3 2.9 copy-start.1
  121.2 1.5 copy-start.2
  121.2 4.3 copy-start.3
  214.7 122.2 %all-to-all-start.1 = ((bf16[32,1,32,2560]{3,2,1,0:T(8,128)(2,1)}), bf16[32,1,32,2560]{3,2,1,0:T(8,128)(2,1)}, u32[]{:S(2)}, u32[]{:S(2)}) async-start(bf16[32,1,32,2560]{3,2,1,0:T(8,128)(2,1)} %bitcast.235), calls=%async_computation.1 | async-start | bytes 10485760 | tf_op jit(solution)/shard_map/all_to_all | solution.py:56
  336.9 4.5 copy-start.6
  341.4 5.4 copy-start.9
  346.8 0.8 copy-start.12
  351.4 12.7 %copy-start.8 = (bf16[2560,32]{0,1:T(8,128)(2,1)S(1)}, bf16[2560,32]{0,1:T(8,128)(2,1)}, u32[]{:S(2)}) copy-start(bf16[2560,32]{0,1:T(8,128)(2,1)} %param.21) | copy-start | bytes 491524
  351.4 125.5 %all-to-all-start.2 = ((bf16[32,1,32,2560]{3,2,1,0:T(8,128)(2,1)}), bf16[32,1,32,2560]{3,2,1,0:T(8,128)(2,1)}, u32[]{:S(2)}, u32[]{:S(2)}) async-start(bf16[32,1,32,2560]{3,2,1,0:T(8,128)(2,1)} %fusion.13), calls=%async_computation.2 | async-start | bytes 10485760 | tf_op jit(solution)/shard_map/all_to_all | solution.py:177
  515.4 176.2 %all-to-all-start.3 = ((bf16[32,1,32,2560]{3,2,1,0:T(8,128)(2,1)}), bf16[32,1,32,2560]{3,2,1,0:T(8,128)(2,1)}, u32[]{:S(2)}, u32[]{:S(2)}) async-start(bf16[32,1,32,2560]{3,2,1,0:T(8,128)(2,1)} %bitcast.236), calls=%async_computation.3 | async-start | bytes 10485760 | tf_op jit(solution)/shard_map/all_to_all | solution.py:56
  525.0 164.4 %all-reduce.6.cloned.1.call-start = ((), (), s32[]{:S(2)}) async-start(), calls=%async_computation.8 | async-start | bytes 2621440 | tf_op jit(solution)/shard_map/psum | solution.py:183
  529.4 460.9 %all-reduce.8.cloned.1.call-start = ((), (), s32[]{:S(2)}) async-start(), calls=%async_computation.9 | async-start | bytes 655360 | tf_op jit(solution)/shard_map/psum | solution.py:193
  691.6 4.1 copy-start.10
  695.8 3.9 copy-start.11
  748.0 2.5 copy-start.13
Sparse Core Ops, SparseCore 0:
  49.1 64.4 all-gather.2
  122.8 86.1 all-reduce.3
  529.6 159.7 all-reduce.5
  692.4 297.9 all-reduce.7
where the time goes:
time: 1000 us; the launch traced here: 999 us
  waiting for transfers between devices  707 us (71%)
  blocking collectives  75.3 us (8%)
  local copies, waits for them, and re-layouts  60.3 us (6%)
  matrix products  58.1 us (6%)
  other arithmetic  47.3 us (5%)
  starting transfers between devices  36.6 us (4%)
  between operations  14.2 us (1%)
    psum x1, waiting for transfers between devices, local(): router_grad = lax.psum(router_term, ('dp', 'ctx'))  189 us
    psum x1, waiting for transfers between devices, local(): moe, dweight = lax.psum((moe_part, dweight_part), 'exp')  158 us
    all_to_all x2, waiting for transfers between devices, route_slots(): lax.all_to_all(outgoing, ('dp', 'ctx'), split_axis=0, concat_axis=0, tile...  113 us
    all_to_all x1, waiting for transfers between devices, local(): lax.all_to_all(expert_part, ('dp', 'ctx'), split_axis=0, concat_axis=0, t...  107 us
    psum x1, waiting for transfers between devices, local(): attention = lax.psum(head_part, 'exp')  83 us
    all_gather x1, blocking collectives, local(): lax.all_gather(doc_ids[0], 'ctx', axis=0, tiled=True)  37.8 us
    unnamed x2, other arithmetic  33.5 us
    all_to_all x1, waiting for transfers between devices, from_everyone(): lax.all_to_all(jnp.broadcast_to(array[None], (count, *array.shape)), axis...  29.8 us
  transfers between devices with their start and end apart: 8, of which 7 were waited for; matrix products, arithmetic and copies ran while one was open for 11% of the time, Pallas kernels for 0%

commit v1 on v0

--- a/solution.py
+++ b/solution.py
@@ -190,7 +190,7 @@
     dprobs = jnp.sum(id_hits * dchosen[:, :, None], axis=1)
     dlogits = router_probs * (dprobs - jnp.sum(router_probs * dprobs, axis=1, keepdims=True))
     router_term = jnp.dot(normed.astype(jnp.float32).T, dlogits, precision=lax.Precision.HIGHEST)
-    router_grad = lax.psum(router_term, ("dp", "ctx"))
+    router_grad = jnp.sum(lax.all_gather(router_term, ("dp", "ctx")), axis=0)
     slot_cot = jnp.einsum(
         "se,sd->ed", combine, cot_rows, preferred_element_type=jnp.float32
     ).astype(jnp.bfloat16)

time: 1000 us -> 832 us (0.83)
  waiting for transfers between devices: 707 us -> 520 us
    psum x1 -> x0, waiting for transfers between devices: 189 us -> none  [local(): router_grad = lax.psum(router_term, ('dp', 'ctx'))]
    unnamed x40 -> x38, local copies, waits for them, and re-layouts: 23.9 us -> 32.2 us
  transfers between devices with their start and end apart: 8 -> 8, of which waited for: 7 -> 6; matrix products, arithmetic and copies ran while one was open for 11% -> 14% of each run, Pallas kernels for 0% -> 0%
where the time goes in v1:
time: 832 us; the launch traced here: 821 us
  waiting for transfers between devices  520 us (62%)
  blocking collectives  76.1 us (9%)
  local copies, waits for them, and re-layouts  66.9 us (8%)
  matrix products  57.4 us (7%)
  other arithmetic  49.8 us (6%)
  starting transfers between devices  36.7 us (4%)
  between operations  14.5 us (2%)
    psum x1, waiting for transfers between devices, local(): moe, dweight = lax.psum((moe_part, dweight_part), 'exp')  160 us
    all_to_all x2, waiting for transfers between devices, route_slots(): lax.all_to_all(outgoing, ('dp', 'ctx'), split_axis=0, concat_axis=0, tile...  113 us
    all_to_all x1, waiting for transfers between devices, local(): lax.all_to_all(expert_part, ('dp', 'ctx'), split_axis=0, concat_axis=0, t...  108 us
    psum x1, waiting for transfers between devices, local(): attention = lax.psum(head_part, 'exp')  83 us
    all_gather x1, blocking collectives, local(): lax.all_gather(doc_ids[0], 'ctx', axis=0, tiled=True)  37.8 us
    unnamed x2, other arithmetic  33.7 us
    unnamed x38, local copies, waits for them, and re-layouts  32.2 us
    all_to_all x1, waiting for transfers between devices, from_everyone(): lax.all_to_all(jnp.broadcast_to(array[None], (count, *array.shape)), axis...  29.8 us
  transfers between devices with their start and end apart: 8, of which 6 were waited for; matrix products, arithmetic and copies ran while one was open for 14% of the time, Pallas kernels for 0%

profile of v1, /device:TPU:88, one launch (start us, length us, event | category | flops | bytes accessed | tf_op | source)
XLA Modules:
  0.0 821.3 jit_solution(15162920932063858998)
XLA Ops:
  10.4 5.8 all-to-all-start
  16.3 29.8 %all-to-all-done = f32[8,128,576]{1,2,0:T(8,128)} async-done(((f32[8,128,576]{1,2,0:T(8,128)}), f32[8,128,576]{1,2,0:T(8,128)}, u32[]{:S(2)}, u32[]{:S(2)}) %all-to-all-start) | async-done | bytes 2359328 | tf_op jit(solution)/shard_map/all_to_all | solution.py:13
  46.0 1.8 reduce_sum.111
  49.0 37.8 %all-gather = s32[1,2048]{1,0:T(1,128)S(1)} all-gather(s32[1,128]{1,0:T(1,128)S(1)} %copy-done.4), channel_id=2, replica_groups=mesh['dp'=2,'ctx'=16,'exp'=8] {'ctx'}, dimensions={1}, use_global_device_ids=true | all-gather | bytes 8704 | tf_op jit(solution)/shard_map/all_gather | solution.py:93
  87.1 26.5 %all-gather.5.cloned.1.call-done = bf16[2048,576]{0,1:T(8,128)(2,1)} async-done(((bf16[128,576]{0,1:T(8,128)(2,1)}), bf16[2048,576]{0,1:T(8,128)(2,1)}) %all-gather.5.cloned.1.call-update) | async-done | bytes 2359312 | tf_op jit(solution)/shard_map/all_gather | solution.py:92
  113.6 2.7 fusion.51
  116.3 1.9 fusion.156
  118.3 2.9 fusion.72
  123.1 1.7 reduce-window.6
  126.0 83.0 %all-reduce.3.cloned.1.call-done = f32[128,2560]{1,0:T(8,128)} async-done(((f32[128,2560]{1,0:T(8,128)}), f32[128,2560]{1,0:T(8,128)}) %all-reduce.3.cloned.1.call-update) | async-done | bytes 1310736 | tf_op jit(solution)/shard_map/psum | solution.py:124
  209.0 1.8 fusion.64
  210.8 3.9 convolution_convert_fusion.2
  214.7 8.9 %all-to-all-start.1 = ((bf16[32,1,32,2560]{3,2,1,0:T(8,128)(2,1)}), bf16[32,1,32,2560]{3,2,1,0:T(8,128)(2,1)}, u32[]{:S(2)}, u32[]{:S(2)}) async-start(bf16[32,1,32,2560]{3,2,1,0:T(8,128)(2,1)} %bitcast.240), calls=%async_computation.1 | async-start | bytes 10485760 | tf_op jit(solution)/shard_map/all_to_all | solution.py:56
  223.7 113.2 %all-to-all-done.1 = bf16[32,1,32,2560]{3,2,1,0:T(8,128)(2,1)} async-done(((bf16[32,1,32,2560]{3,2,1,0:T(8,128)(2,1)}), bf16[32,1,32,2560]{3,2,1,0:T(8,128)(2,1)}, u32[]{:S(2)}, u32[]{:S(2)}) %all-to-all-start.1) | async-done | bytes 5242912 | tf_op jit(solution)/shard_map/all_to_all | solution.py:56
  336.8 4.5 fusion.55
  341.3 5.4 multiply_convert_fusion.2
  347.5 3.9 fusion.13
  351.4 12.2 %all-to-all-start.2 = ((bf16[32,1,32,2560]{3,2,1,0:T(8,128)(2,1)}), bf16[32,1,32,2560]{3,2,1,0:T(8,128)(2,1)}, u32[]{:S(2)}, u32[]{:S(2)}) async-start(bf16[32,1,32,2560]{3,2,1,0:T(8,128)(2,1)} %fusion.13), calls=%async_computation.2 | async-start | bytes 10485760 | tf_op jit(solution)/shard_map/all_to_all | solution.py:177
  364.7 5.1 gather_fusion
  370.1 107.6 %all-to-all-done.2 = bf16[32,1,32,2560]{3,2,1,0:T(8,128)(2,1)} async-done(((bf16[32,1,32,2560]{3,2,1,0:T(8,128)(2,1)}), bf16[32,1,32,2560]{3,2,1,0:T(8,128)(2,1)}, u32[]{:S(2)}, u32[]{:S(2)}) %all-to-all-start.2) | async-done | bytes 5242912 | tf_op jit(solution)/shard_map/all_to_all | solution.py:177
  477.7 4.1 convolution_bitcast_fusion
  481.8 5.1 gather_fusion.1
  487.2 23.5 %psum.23 = f32[128,6]{0,1:T(8,128)S(1)} all-reduce(f32[128,6]{0,1:T(8,128)S(1)} %and_select_fusion), channel_id=1, replica_groups=mesh['dp'=2,'ctx'=16,'exp'=8] {'exp'}, use_global_device_ids=true, to_apply=%region_15.16 | all-reduce | flops 768 | bytes 6144 | tf_op jit(solution)/shard_map/psum | solution.py:183
  511.1 4.4 fusion.159
  517.0 5.0 convolution_convert_fusion
  522.0 9.6 %all-to-all-start.3 = ((bf16[32,1,32,2560]{3,2,1,0:T(8,128)(2,1)}), bf16[32,1,32,2560]{3,2,1,0:T(8,128)(2,1)}, u32[]{:S(2)}, u32[]{:S(2)}) async-start(bf16[32,1,32,2560]{3,2,1,0:T(8,128)(2,1)} %bitcast.241), calls=%async_computation.3 | async-start | bytes 10485760 | tf_op jit(solution)/shard_map/all_to_all | solution.py:56
  531.6 159.9 %all-reduce.5.cloned.1.call-done = f32[128,2560]{1,0:T(8,128)} async-done(((f32[128,2560]{1,0:T(8,128)}), f32[128,2560]{1,0:T(8,128)}) %all-reduce.5.cloned.1.call-update) | async-done | bytes 1310736 | tf_op jit(solution)/shard_map/psum | solution.py:183
  691.4 2.3 fusion.86
  693.7 4.1 fusion.61
  697.9 3.9 fusion.38
  701.7 3.8 fusion.35
  707.0 8.9 %copy.117 = bf16[1,2560,384]{2,0,1:T(2,128)(2,1)} copy(bf16[1,2560,384]{1,2,0:T(8,128)(2,1)} %pad_maximum_fusion) | data formatting | bytes 3932160 | tf_op jit(solution)/shard_map/concatenate | solution.py:24
  716.5 18.3 %reduce.3 = bf16[2560,384]{1,0:T(8,128)(2,1)} reduce(bf16[2560,1,384]{2,1,0:T(2,128)(2,1)} %bitcast.242, bf16[]{:T(256)} %broadcast.489), dimensions={1}, to_apply=%bitcast.217.reduce_sub_computation | reduce | bytes 3932162
  734.8 2.8 reshape.426
  737.6 8.7 %all_to_all.50 = bf16[2,2,245760]{2,1,0:T(2,128)(2,1)} all-to-all(bf16[2,2,245760]{2,1,0:T(2,128)(2,1)} %reshape.426), channel_id=1, replica_groups=mesh['dp'=2,'ctx'=16,'exp'=8] {'dp'}, dimensions={0} | all-to-all | bytes 3932160 | tf_op jit(solution)/shard_map/all_to_all | solution.py:26
  746.3 4.2 reshape.427
  750.4 2.4 copy.128
  754.5 2.3 copy.120
  758.2 4.1 fusion.32
  762.3 4.5 copy.118
  766.8 15.4 %reduce.4 = bf16[2560,192]{1,0:T(8,128)(2,1)S(1)} reduce(bf16[2560,1,192]{2,1,0:T(2,128)(2,1)} %bitcast.247, bf16[]{:T(256)} %broadcast.489), dimensions={1}, to_apply=%bitcast.219.reduce_sub_computation | reduce | bytes 1966082
  782.3 2.3 reshape.428
  784.6 6.1 all_to_all.51
  790.7 2.9 reshape.429
  793.6 5.1 copy.119
  800.0 2.2 copy.122
  802.2 10.0 %copy.130 = f32[4,8,32,2560]{3,2,1,0:T(8,128)S(1)} copy(f32[4,8,32,2560]{3,1,2,0:T(8,128)} %bitcast.246) | data formatting | bytes 20971520
  812.3 2.3 bitcast_reduce_fusion
  (87 shorter events, 17.9 us)
Async XLA Ops:
  7.2 340.3 %copy-start = (bf16[2,192,2560]{2,1,0:T(8,128)(2,1)S(1)}, bf16[2,192,2560]{2,1,0:T(8,128)(2,1)}, u32[]{:S(2)}) copy-start(bf16[2,192,2560]{2,1,0:T(8,128)(2,1)} %param.26) | copy-start | bytes 5898244
  10.4 5.9 copy-start.5
  10.4 35.7 %all-to-all-start = ((f32[8,128,576]{1,2,0:T(8,128)}), f32[8,128,576]{1,2,0:T(8,128)}, u32[]{:S(2)}, u32[]{:S(2)}) async-start(f32[8,128,576]{1,2,0:T(8,128)} %broadcast_in_dim.34), calls=%async_computation | async-start | bytes 4718592 | tf_op jit(solution)/shard_map/all_to_all | solution.py:13
  16.1 32.8 %copy-start.4 = (s32[1,128]{1,0:T(1,128)S(1)}, s32[1,128]{1,0:T(1,128)}, u32[]{:S(2)}) copy-start(s32[1,128]{1,0:T(1,128)} %param.23) | copy-start | bytes 1540
  16.2 97.4 %copy-start.7 = (bf16[1,128,2,576]{1,3,2,0:T(8,128)(2,1)S(1)}, bf16[1,128,2,576]{1,3,2,0:T(8,128)(2,1)}, u32[]{:S(2)}) copy-start(bf16[1,128,2,576]{1,3,2,0:T(8,128)(2,1)} %param.15) | copy-start | bytes 884740
  16.2 97.4 %all-gather.5.cloned.1.call-start = ((), (), s32[]{:S(2)}) async-start(), calls=%async_computation.6 | async-start | bytes 2506752 | tf_op jit(solution)/shard_map/all_gather | solution.py:92
  48.9 160.1 %all-reduce.3.cloned.1.call-start = ((), (), s32[]{:S(2)}) async-start(), calls=%async_computation.7 | async-start | bytes 2621440 | tf_op jit(solution)/shard_map/psum | solution.py:124
  118.3 2.9 copy-start.1
  121.2 1.5 copy-start.2
  121.2 4.2 copy-start.3
  214.7 122.1 %all-to-all-start.1 = ((bf16[32,1,32,2560]{3,2,1,0:T(8,128)(2,1)}), bf16[32,1,32,2560]{3,2,1,0:T(8,128)(2,1)}, u32[]{:S(2)}, u32[]{:S(2)}) async-start(bf16[32,1,32,2560]{3,2,1,0:T(8,128)(2,1)} %bitcast.240), calls=%async_computation.1 | async-start | bytes 10485760 | tf_op jit(solution)/shard_map/all_to_all | solution.py:56
  336.8 4.5 copy-start.6
  341.3 5.4 copy-start.9
  346.7 0.8 copy-start.12
  351.4 12.8 %copy-start.8 = (bf16[2560,32]{0,1:T(8,128)(2,1)S(1)}, bf16[2560,32]{0,1:T(8,128)(2,1)}, u32[]{:S(2)}) copy-start(bf16[2560,32]{0,1:T(8,128)(2,1)} %param.21) | copy-start | bytes 491524
  351.4 126.3 %all-to-all-start.2 = ((bf16[32,1,32,2560]{3,2,1,0:T(8,128)(2,1)}), bf16[32,1,32,2560]{3,2,1,0:T(8,128)(2,1)}, u32[]{:S(2)}, u32[]{:S(2)}) async-start(bf16[32,1,32,2560]{3,2,1,0:T(8,128)(2,1)} %fusion.13), calls=%async_computation.2 | async-start | bytes 10485760 | tf_op jit(solution)/shard_map/all_to_all | solution.py:177
  363.6 327.8 %all-reduce.5.cloned.1.call-start = ((), (), s32[]{:S(2)}) async-start(), calls=%async_computation.8 | async-start | bytes 2621440 | tf_op jit(solution)/shard_map/psum | solution.py:183
  515.6 286.6 %all-gather.7.cloned.1.call-start = ((), (), s32[]{:S(2)}) async-start(), calls=%async_computation.9 | async-start | bytes 10813440 | tf_op jit(solution)/shard_map/all_gather | solution.py:193
  522.0 171.8 %all-to-all-start.3 = ((bf16[32,1,32,2560]{3,2,1,0:T(8,128)(2,1)}), bf16[32,1,32,2560]{3,2,1,0:T(8,128)(2,1)}, u32[]{:S(2)}, u32[]{:S(2)}) async-start(bf16[32,1,32,2560]{3,2,1,0:T(8,128)(2,1)} %bitcast.241), calls=%async_computation.3 | async-start | bytes 10485760 | tf_op jit(solution)/shard_map/all_to_all | solution.py:56
  693.7 4.1 copy-start.10
  697.8 3.9 copy-start.11
Sparse Core Ops, SparseCore 0:
  49.1 64.4 all-gather.4
  122.8 86.1 all-reduce.2
  515.7 175.6 all-reduce.4
  694.4 87.5 all-gather.6
